TPU v7x, 512 devices: a whole 4x4x16 slice. The times are simulated.
512 devices in a mesh: mem: 16 (over z), sp: 32 (over x, y, core).
Axes of the slice: x: 4, y: 4, z: 16, core: 2. Of those that a mesh axis runs over, the one named last changes fastest.
Arguments:
- ensemble: bfloat16 [256, 131072], P('mem', 'sp'), may hold values from -6 to 6
- predicted: bfloat16 [256, 65536], P('mem', 'sp'), may hold values from -2 to 2
- observed: float32 [65536], P('sp'), may hold values from -6 to 6
- perturbation: bfloat16 [256, 65536], P('mem', 'sp'), may hold values from -6 to 6
- noise_variance: float32 [512], P('sp'), may hold values from 0.25 to 4
- block_lists: int32 [32, 64], P('sp'), may hold values from 0 to 511, as said below
- localization: int32 [1024, 64], P('sp'), may hold values 0 or 1
Outputs:
- increment: float32 [256, 131072], P('mem', 'sp')
Inputs may be any that keep to these rules, and one draw needn't show every extreme that they name: `block_lists`: row t lists the 64 distinct data blocks used by the bricks of index t of sp, in increasing order; block j is held by index j // 16; a row uses 1 to 3 blocks of each holder, exactly 3 of some holder, and every holder gives 3 blocks to some row.
All inputs are finite; a program needn't handle non-finite values. No bound on the sum of `localization` on one device may be relied on, other than what follows from the above.
Results may differ from a plain program's by a relative error of at most 0.0055.
Values may be sent and summed in bfloat16 or wider, within the bound.
No kernel may reach another device: no remote copies, remote signals or barrier semaphores. Data moves between devices by JAX's collectives and lax.ppermute only.
A program may use at most 64 MiB of HBM per device.

v0:
```python
import jax
import jax.numpy as jnp
from jax import lax
from jax.sharding import PartitionSpec as P

SLOTS = 3
ENSEMBLE_SCALE = 2.0**13
PREDICTED_SCALE = 2.0**14


def per_device(
    ensemble, predicted, observed, perturbation, noise_variance, block_lists, localization
):
    bf16, f16, f32 = (jnp.bfloat16, jnp.float16, jnp.float32)
    mem, sp = (lax.axis_size("mem"), lax.axis_size("sp"))
    local = ensemble.shape[0]
    members = local * mem
    cells = ensemble.shape[1]
    bricks = localization.shape[0]
    brick = cells // bricks
    blocks = noise_variance.shape[0]
    data = predicted.shape[1]
    block = data // blocks
    need = block_lists.shape[1]
    needed = block_lists[0]
    holder = needed // blocks
    before = jnp.sum(needed[None, :] < (holder * blocks)[:, None], axis=1)
    slot = holder * SLOTS + (jnp.arange(need) - before)
    slot_hot = slot[:, None] == jnp.arange(sp * SLOTS)[None, :]
    asked = jnp.sum(jnp.where(slot_hot, (needed % blocks)[:, None], 0), axis=0)
    asked = jnp.pad(asked.reshape(sp, SLOTS), ((0, 0), (0, 128 - SLOTS)))
    wanted = lax.all_to_all(asked, "sp", split_axis=0, concat_axis=0, tiled=True)
    wanted = wanted[:, :SLOTS].reshape(-1)
    slot_pattern = jnp.dot(
        localization.astype(bf16), slot_hot.astype(bf16), preferred_element_type=f32
    ).astype(bf16)
    sent = jnp.concatenate(
        [
            (predicted.astype(f32) * PREDICTED_SCALE).astype(f16),
            (ensemble.astype(f32) * ENSEMBLE_SCALE).astype(f16),
        ],
        axis=1,
    )
    whole = lax.all_gather(sent, "mem", axis=0, tiled=True)
    whole_predicted = whole[:, :data].astype(f32)
    whole_ensemble = whole[:, data:].astype(f32)
    data_mean = jnp.sum(whole_predicted, axis=0) / members
    data_anomalies = (whole_predicted - data_mean).astype(bf16)
    variance = jnp.repeat(noise_variance, block)
    innovation = (
        observed[None, :] + jnp.sqrt(variance) * perturbation.astype(f32) - predicted.astype(f32)
    )
    weighted = (innovation / variance).astype(bf16)
    products = jnp.einsum(
        "njd,mjd->jnm",
        weighted.reshape(local, blocks, block),
        data_anomalies.reshape(members, blocks, block),
        preferred_element_type=f32,
    ).astype(bf16)
    picked = (wanted[:, None] == jnp.arange(blocks)[None, :]).astype(bf16)
    chosen = jnp.einsum("sj,jnm->snm", picked, products, preferred_element_type=f32).astype(bf16)
    chosen = chosen.reshape(sp, SLOTS * local, members)
    got = lax.all_to_all(chosen, "sp", split_axis=0, concat_axis=0, tiled=True)
    got = got.reshape(sp * SLOTS, local, members)
    gains = jnp.einsum("bs,snm->bnm", slot_pattern, got, preferred_element_type=f32).astype(bf16)
    model_mean = jnp.sum(whole_ensemble, axis=0) / members
    model_anomalies = (whole_ensemble - model_mean).astype(bf16)
    increment = jnp.einsum(
        "bnm,mbc->nbc",
        gains,
        model_anomalies.reshape(members, bricks, brick),
        preferred_element_type=f32,
    )
    return increment.reshape(local, cells) / ((members - 1) * (ENSEMBLE_SCALE * PREDICTED_SCALE))


def solution(mesh):
    in_specs = (
        P("mem", "sp"),
        P("mem", "sp"),
        P("sp"),
        P("mem", "sp"),
        P("sp"),
        P("sp", None),
        P("sp", None),
    )
    return jax.shard_map(
        per_device, mesh=mesh, in_specs=in_specs, out_specs=P("mem", "sp"), check_vma=False
    )
```

profile of v0, /device:TPU:1, one launch (start us, length us, event | category | flops | bytes accessed | tf_op | source)
XLA Modules:
  0.0 100.3 jit_solution(8255561236363733523)
XLA Ops:
  0.0 0.7 broadcast_multiply_fusion.2
  0.7 0.8 convert_reduce_fusion.2
  1.5 0.1 select_reduce_fusion
  1.6 0.1 reshape.108
  1.7 0.6 pad.4
  2.3 10.4 %all-to-all-start = ((s32[32,1,128]{2,1,0:T(1,128)}), s32[32,1,128]{2,1,0:T(1,128)S(1)}, u32[]{:S(2)}, u32[]{:S(2)}) async-start(s32[32,1,128]{2,1,0:T(1,128)} %bitcast.3), calls=%async_computation | async-start | bytes 32768 | tf_op jit(solution)/shard_map/all_to_all | solution.py:32
  12.7 0.7 bitcast_sqrt_fusion
  13.4 0.7 broadcast_bitcast_fusion
  14.2 0.9 multiply_convert_fusion
  15.1 0.9 fusion.24
  16.0 0.1 pad_maximum_fusion
  16.1 50.7 %all-gather.1 = f16[256,6144]{1,0:T(8,128)(2,1)S(1)} all-gather(f16[16,6144]{1,0:T(8,128)(2,1)S(1)} %pad_maximum_fusion), channel_id=1, replica_groups=mesh['mem'=16,'sp'=32] {'mem'}, dimensions={0}, use_global_device_ids=true | all-gather | bytes 3342336 | tf_op jit(solution)/shard_map/all_gather | solution.py:44
  66.8 0.2 convert_reduce_fusion.1
  67.0 0.4 convolution_convert_fusion.2
  67.3 0.0 all-to-all-done
  67.4 0.1 eq.33
  67.5 0.4 convolution_convert_fusion
  67.9 1.3 %copy.33 = bf16[96,16,256]{2,1,0:T(8,128)(2,1)} copy(bf16[96,16,256]{2,0,1:T(8,128)(2,1)S(1)} %convolution_convert_fusion) | data formatting | bytes 1572864 | tf_op jit(solution)/shard_map/convert_element_type | solution.py:61
  69.2 13.9 %all-to-all-start.1 = ((bf16[32,48,256]{2,1,0:T(8,128)(2,1)}), bf16[32,48,256]{2,1,0:T(8,128)(2,1)}, u32[]{:S(2)}, u32[]{:S(2)}) async-start(bf16[32,48,256]{2,1,0:T(8,128)(2,1)} %bitcast.54), calls=%async_computation.1 | async-start | bytes 1572864 | tf_op jit(solution)/shard_map/all_to_all | solution.py:63
  83.1 0.3 convert_reduce_fusion
  83.4 14.0 %all-to-all-done.1 = bf16[32,48,256]{2,1,0:T(8,128)(2,1)} async-done(((bf16[32,48,256]{2,1,0:T(8,128)(2,1)}), bf16[32,48,256]{2,1,0:T(8,128)(2,1)}, u32[]{:S(2)}, u32[]{:S(2)}) %all-to-all-start.1) | async-done | bytes 786464 | tf_op jit(solution)/shard_map/all_to_all | solution.py:63
  97.4 1.6 %convolution_convert_fusion.1 = bf16[32,16,256]{2,0,1:T(8,128)(2,1)S(1)} fusion(bf16[96,16,256]{2,1,0:T(8,128)(2,1)} %bitcast.8, s32[64]{0:T(128)S(1)} %subtract_add_fusion, s32[32,64]{1,0:T(8,128)S(1)} %copy-done), kind=kOutput, calls=%fused_computation.11 | convolution fusion | flops 25701376 | bytes 1057024 | tf_op jit(solution)/shard_map/bs,snm->bnm/dot_general | solution.py:65
  99.0 0.6 fusion.9
  99.5 0.7 copy.65
  (5 shorter events, 0.0 us)
Async XLA Ops:
  2.3 65.0 %all-to-all-start = ((s32[32,1,128]{2,1,0:T(1,128)}), s32[32,1,128]{2,1,0:T(1,128)S(1)}, u32[]{:S(2)}, u32[]{:S(2)}) async-start(s32[32,1,128]{2,1,0:T(1,128)} %bitcast.3), calls=%async_computation | async-start | bytes 32768 | tf_op jit(solution)/shard_map/all_to_all | solution.py:32
  67.3 30.0 %copy-start = (s32[32,64]{1,0:T(8,128)S(1)}, s32[32,64]{1,0:T(8,128)}, u32[]{:S(2)}) copy-start(s32[32,64]{1,0:T(8,128)} %param.13) | copy-start | bytes 24580
  69.2 28.2 %all-to-all-start.1 = ((bf16[32,48,256]{2,1,0:T(8,128)(2,1)}), bf16[32,48,256]{2,1,0:T(8,128)(2,1)}, u32[]{:S(2)}, u32[]{:S(2)}) async-start(bf16[32,48,256]{2,1,0:T(8,128)(2,1)} %bitcast.54), calls=%async_computation.1 | async-start | bytes 1572864 | tf_op jit(solution)/shard_map/all_to_all | solution.py:63
where the time goes:
time: 101 us; the launch traced here: 100 us
  blocking collectives  50.7 us (50%)
  starting transfers between devices  24.2 us (24%)
  waiting for transfers between devices  14 us (14%)
  local copies, waits for them, and re-layouts  4.36 us (4%)
  other arithmetic  4 us (4%)
  matrix products  2.93 us (3%)
    all_gather x1, blocking collectives, per_device(): whole = lax.all_gather(sent, 'mem', axis=0, tiled=True)  50.7 us
    all_to_all x1, waiting for transfers between devices, per_device(): got = lax.all_to_all(chosen, 'sp', split_axis=0, concat_axis=0, tiled=True)  14 us
    all_to_all x1, starting transfers between devices, per_device(): got = lax.all_to_all(chosen, 'sp', split_axis=0, concat_axis=0, tiled=True)  13.9 us
    all_to_all x1, starting transfers between devices, per_device(): lax.all_to_all(asked, 'sp', split_axis=0, concat_axis=0, tiled=True)  10.4 us
  transfers between devices with their start and end apart: 2, of which 1 were waited for; matrix products, arithmetic and copies ran while one was open for 4% of the time, Pallas kernels for 0%

commit v1 on v0

--- a/solution.py
+++ b/solution.py
@@ -6,6 +6,13 @@
 SLOTS = 3
 ENSEMBLE_SCALE = 2.0**13
 PREDICTED_SCALE = 2.0**14
+
+
+def all_by_exchange(x, axis, dim):
+    size = lax.axis_size(axis)
+    pieces = jnp.stack([x for _ in range(size)])
+    pieces = lax.all_to_all(pieces, axis, split_axis=0, concat_axis=0)
+    return jnp.concatenate(pieces, axis=dim)
 
 
 def per_device(
@@ -41,7 +48,7 @@
         ],
         axis=1,
     )
-    whole = lax.all_gather(sent, "mem", axis=0, tiled=True)
+    whole = all_by_exchange(sent, "mem", 0)
     whole_predicted = whole[:, :data].astype(f32)
     whole_ensemble = whole[:, data:].astype(f32)
     data_mean = jnp.sum(whole_predicted, axis=0) / members

time: 101 us -> 200 us (1.98)
  waiting for transfers between devices: 14 us -> 150 us
  blocking collectives: 50.7 us -> 0 us
  starting transfers between devices: 24.2 us -> 31.1 us
  local copies, waits for them, and re-layouts: 4.36 us -> 9.64 us
    all_to_all x0 -> x1, waiting for transfers between devices: none -> 137 us  [all_by_exchange(): pieces = lax.all_to_all(pieces, axis, split_axis=0, concat_axis=0)]
    all_gather x1 -> x0, blocking collectives: 50.7 us -> none  [per_device(): whole = lax.all_gather(sent, 'mem', axis=0, tiled=True)]
    all_to_all x0 -> x1, starting transfers between devices: none -> 13 us  [all_by_exchange(): pieces = lax.all_to_all(pieces, axis, split_axis=0, concat_axis=0)]
    all_to_all x1, starting transfers between devices: 13.9 us -> 7.74 us  [per_device(): got = lax.all_to_all(chosen, 'sp', split_axis=0, concat_axis=0, tiled=True)]
    all_to_all x1, waiting for transfers between devices: 14 us -> 9.3 us  [per_device(): got = lax.all_to_all(chosen, 'sp', split_axis=0, concat_axis=0, tiled=True)]
    all_to_all x1, waiting for transfers between devices: 0.01 us -> 3.59 us  [per_device(): lax.all_to_all(asked, 'sp', split_axis=0, concat_axis=0, tiled=True)]
    convert_element_type x0 -> x1, local copies, waits for them, and re-layouts: none -> 3.28 us  [per_device(): model_anomalies = (whole_ensemble - model_mean).astype(bf16)]
    another operation x0 -> x1, local copies, waits for them, and re-layouts: none -> 2.03 us  [all_by_exchange(): pieces = jnp.stack([x for _ in range(size)])]
  transfers between devices with their start and end apart: 2 -> 3, of which waited for: 1 -> 3; matrix products, arithmetic and copies ran while one was open for 4% -> 4% of each run, Pallas kernels for 0% -> 0%
where the time goes in v1:
time: 200 us; the launch traced here: 199 us
  waiting for transfers between devices  150 us (75%)
  starting transfers between devices  31.1 us (16%)
  local copies, waits for them, and re-layouts  9.64 us (5%)
  other arithmetic  5.79 us (3%)
  matrix products  3.04 us (2%)
    all_to_all x1, waiting for transfers between devices, all_by_exchange(): pieces = lax.all_to_all(pieces, axis, split_axis=0, concat_axis=0)  137 us
    all_to_all x1, starting transfers between devices, all_by_exchange(): pieces = lax.all_to_all(pieces, axis, split_axis=0, concat_axis=0)  13 us
    all_to_all x1, starting transfers between devices, per_device(): lax.all_to_all(asked, 'sp', split_axis=0, concat_axis=0, tiled=True)  10.4 us
    all_to_all x1, waiting for transfers between devices, per_device(): got = lax.all_to_all(chosen, 'sp', split_axis=0, concat_axis=0, tiled=True)  9.3 us
    all_to_all x1, starting transfers between devices, per_device(): got = lax.all_to_all(chosen, 'sp', split_axis=0, concat_axis=0, tiled=True)  7.74 us
  transfers between devices with their start and end apart: 3, of which 3 were waited for; matrix products, arithmetic and copies ran while one was open for 4% of the time, Pallas kernels for 0%

profile of v1, /device:TPU:1, one launch (start us, length us, event | category | flops | bytes accessed | tf_op | source)
XLA Modules:
  0.0 199.3 jit_solution(4354237936454875738)
XLA Ops:
  0.0 0.7 broadcast_multiply_fusion.2
  0.7 0.8 convert_reduce_fusion.2
  1.7 0.6 pad.4
  2.3 10.4 %all-to-all-start.1 = ((s32[32,1,128]{2,1,0:T(1,128)}), s32[32,1,128]{2,1,0:T(1,128)S(1)}, u32[]{:S(2)}, u32[]{:S(2)}) async-start(s32[32,1,128]{2,1,0:T(1,128)} %bitcast.5), calls=%async_computation.1 | async-start | bytes 32768 | tf_op jit(solution)/shard_map/all_to_all | solution.py:39
  12.7 0.7 bitcast_sqrt_fusion
  13.4 0.7 broadcast_bitcast_fusion
  14.2 0.9 multiply_convert_fusion
  15.1 0.9 fusion.15
  16.1 3.6 %all-to-all-done.1 = s32[32,1,128]{2,1,0:T(1,128)S(1)} async-done(((s32[32,1,128]{2,1,0:T(1,128)}), s32[32,1,128]{2,1,0:T(1,128)S(1)}, u32[]{:S(2)}, u32[]{:S(2)}) %all-to-all-start.1) | async-done | bytes 16416 | tf_op jit(solution)/shard_map/all_to_all | solution.py:39
  19.7 2.0 %stack.2 = f16[16,16,6144]{2,1,0:T(8,128)(2,1)} broadcast(f16[16,6144]{1,0:T(8,128)(2,1)S(1)} %pad_maximum_fusion), dimensions={1,2} | broadcast | bytes 3342336 | tf_op jit(solution)/shard_map/stack | solution.py:13
  21.7 13.0 %all-to-all-start = ((f16[16,16,6144]{2,1,0:T(8,128)(2,1)}), f16[16,16,6144]{2,1,0:T(8,128)(2,1)S(1)}, u32[]{:S(2)}, u32[]{:S(2)}) async-start(f16[16,16,6144]{2,1,0:T(8,128)(2,1)} %stack.2), calls=%async_computation | async-start | bytes 6291456 | tf_op jit(solution)/shard_map/all_to_all | solution.py:14
  34.9 136.7 %all-to-all-done = f16[16,16,6144]{2,1,0:T(8,128)(2,1)S(1)} async-done(((f16[16,16,6144]{2,1,0:T(8,128)(2,1)}), f16[16,16,6144]{2,1,0:T(8,128)(2,1)S(1)}, u32[]{:S(2)}, u32[]{:S(2)}) %all-to-all-start) | async-done | bytes 3145760 | tf_op jit(solution)/shard_map/all_to_all | solution.py:14
  171.6 0.2 convert_reduce_fusion.1
  171.7 0.3 convert_reduce_fusion
  172.1 0.4 convolution_convert_fusion.2
  172.4 0.4 convolution_convert_fusion
  172.9 1.3 copy.44
  174.2 7.7 %all-to-all-start.2 = ((bf16[32,48,256]{2,1,0:T(8,128)(2,1)}), bf16[32,48,256]{2,1,0:T(8,128)(2,1)}, u32[]{:S(2)}, u32[]{:S(2)}) async-start(bf16[32,48,256]{2,1,0:T(8,128)(2,1)} %bitcast.51), calls=%async_computation.2 | async-start | bytes 1572864 | tf_op jit(solution)/shard_map/all_to_all | solution.py:70
  181.9 1.8 fusion
  183.7 3.3 %copy.39 = bf16[256,4096]{0,1:T(8,128)(2,1)S(1)} copy(bf16[256,4096]{1,0:T(8,128)(2,1)} %fusion) | data formatting | bytes 4194304 | tf_op jit(solution)/shard_map/convert_element_type | solution.py:74
  187.0 9.3 %all-to-all-done.2 = bf16[32,48,256]{2,1,0:T(8,128)(2,1)} async-done(((bf16[32,48,256]{2,1,0:T(8,128)(2,1)}), bf16[32,48,256]{2,1,0:T(8,128)(2,1)}, u32[]{:S(2)}, u32[]{:S(2)}) %all-to-all-start.2) | async-done | bytes 786464 | tf_op jit(solution)/shard_map/all_to_all | solution.py:70
  196.3 1.6 convolution_convert_fusion.1
  197.9 0.7 fusion.2
  198.6 0.7 copy.68
  (9 shorter events, 0.4 us)
Async XLA Ops:
  2.3 17.3 %all-to-all-start.1 = ((s32[32,1,128]{2,1,0:T(1,128)}), s32[32,1,128]{2,1,0:T(1,128)S(1)}, u32[]{:S(2)}, u32[]{:S(2)}) async-start(s32[32,1,128]{2,1,0:T(1,128)} %bitcast.5), calls=%async_computation.1 | async-start | bytes 32768 | tf_op jit(solution)/shard_map/all_to_all | solution.py:39
  21.7 149.8 %all-to-all-start = ((f16[16,16,6144]{2,1,0:T(8,128)(2,1)}), f16[16,16,6144]{2,1,0:T(8,128)(2,1)S(1)}, u32[]{:S(2)}, u32[]{:S(2)}) async-start(f16[16,16,6144]{2,1,0:T(8,128)(2,1)} %stack.2), calls=%async_computation | async-start | bytes 6291456 | tf_op jit(solution)/shard_map/all_to_all | solution.py:14
  174.2 22.1 %all-to-all-start.2 = ((bf16[32,48,256]{2,1,0:T(8,128)(2,1)}), bf16[32,48,256]{2,1,0:T(8,128)(2,1)}, u32[]{:S(2)}, u32[]{:S(2)}) async-start(bf16[32,48,256]{2,1,0:T(8,128)(2,1)} %bitcast.51), calls=%async_computation.2 | async-start | bytes 1572864 | tf_op jit(solution)/shard_map/all_to_all | solution.py:70
  183.7 12.6 %copy-start = (s32[32,64]{1,0:T(8,128)S(1)}, s32[32,64]{1,0:T(8,128)}, u32[]{:S(2)}) copy-start(s32[32,64]{1,0:T(8,128)} %param.13) | copy-start | bytes 24580
